TPU v7x, 512 devices: a whole 4x8x8 slice. The times are simulated.
512 devices in a mesh: row: 32 (over y_hi, z, core), col: 16 (over y_lo, x).
Axes of the slice: x: 4, y: 8 (y_hi: 2, y_lo: 4; y = y_hi * 4 + y_lo), z: 8, core: 2. Of those that a mesh axis runs over, the one named last changes fastest.
Arguments:
- stress: float32 [256, 16384], P('col', 'row'), may hold values from -2.5 to 2.5
- state: float32 [256, 8192], P('col', 'row'), may hold values from 0 to 1
- load_rate: int32 [256, 16384], P('col', 'row'), may hold values from 0 to 2047
- a_param: float32 [8192], P('row'), may hold values from 1 to 2
- b_param: float32 [8192], P('row'), may hold values from 0.25 to 1
- near_band: bfloat16 [16384, 768], P('row'), may hold values from -0.21875 to 0.21875
- u_far: bfloat16 [64, 64, 32, 256], P('row', 'col'), may hold values from -0.1875 to 0.1875
- v_far: bfloat16 [64, 64, 32, 256], P('row', 'col'), may hold values from -0.375 to 0.375
- ranks: int32 [64, 64], P('row', 'col'), may hold values from 1 to 32, as said below
Outputs:
- new_stress: float32 [256, 16384], P('col', 'row')
- new_state: float32 [256, 8192], P('col', 'row')
Inputs may be any that keep to these rules, and one draw needn't show every extreme that they name: ranks of blocks with |I - J| <= 1 are not used; blocks with |I - J| = 2 have rank 32.
All inputs are finite; a program needn't handle non-finite values.
Results may differ from a plain program's by a relative error of at most 0.0021.
Values may be sent and summed in bfloat16 or wider, within the bound.
No kernel may reach another device: no remote copies, remote signals or barrier semaphores. Data moves between devices by JAX's collectives and lax.ppermute only.
A program may use at most 64 MiB of HBM per device.

v0:
```python
import jax
import jax.numpy as jnp
from jax import lax
from jax.sharding import PartitionSpec as P

B = 128
HSTEP = 0.2
RATE_UNIT = 1.0 / 1024.0


def broadcast(value, axis, source):
    kept = jnp.where(lax.axis_index(axis) == source, value, 0).astype(value.dtype)
    return lax.psum(kept, axis)


def extended(cells, sides, width):
    for axis, dim in sides:
        count = lax.axis_size(axis)
        ends = count - 1
        head = lax.slice_in_dim(cells, 0, width, axis=dim)
        tail = lax.slice_in_dim(cells, cells.shape[dim] - width, cells.shape[dim], axis=dim)
        cells = jnp.concatenate(
            [
                lax.ppermute(tail, axis, [(i, (i + 1) % count) for i in range(ends)]),
                cells,
                lax.ppermute(head, axis, [((i + 1) % count, i) for i in range(ends)]),
            ],
            axis=dim,
        )
    return cells


def rates_and_drift(stress_now, state_now, plate_rate, a_param, b_param):
    members = stress_now.shape[0]
    block_count = a_param.shape[0] // B
    stress_view = stress_now.reshape(members, block_count, 2, B)
    state_view = state_now.reshape(members, block_count, 1, B)
    direct_view = a_param.reshape(1, block_count, 1, B)
    evolve_view = b_param.reshape(1, block_count, B)
    slip_rate = 2.0 * jnp.exp(-state_view) * jnp.sinh(stress_view / direct_view)
    slip_speed = jnp.sqrt(jnp.sum(slip_rate * slip_rate, axis=2))
    drift = evolve_view * (jnp.exp(-state_view[:, :, 0]) - slip_speed)
    excess = (slip_rate - plate_rate.reshape(members, block_count, 2, B)).astype(jnp.bfloat16)
    return (excess.reshape(members, -1), drift.reshape(members, -1))


def far_terms(columns, u_far, v_far, ranks, row_index, col_index):
    block_rows, block_cols, rank_slots, block_dofs = u_far.shape
    members = columns.shape[0]
    grid = columns.reshape(members, block_cols, block_dofs)
    weights = jnp.einsum("mjd,ijrd->ijmr", grid, v_far, preferred_element_type=jnp.float32)
    global_rows = row_index * block_rows + jnp.arange(block_rows, dtype=jnp.int32)
    global_cols = col_index * block_cols + jnp.arange(block_cols, dtype=jnp.int32)
    distant = jnp.abs(global_rows[:, None] - global_cols[None, :]) >= 2
    active = (jnp.arange(rank_slots, dtype=jnp.int32)[None, None, :] < ranks[:, :, None]) & distant[
        :, :, None
    ]
    weights = jnp.where(active[:, :, None, :], weights, 0.0).astype(jnp.bfloat16)
    partial_value = jnp.einsum("ijmr,ijrd->mid", weights, u_far, preferred_element_type=jnp.float32)
    return partial_value.reshape(members, -1)


def near_terms(padded, first_block, near_band):
    block_dofs = near_band.shape[1] // 3
    block_rows = near_band.shape[0] // block_dofs
    members = padded.shape[0]
    segment = lax.dynamic_slice_in_dim(
        padded, first_block * block_dofs, (block_rows + 2) * block_dofs, 1
    )
    segment = segment.reshape(members, block_rows + 2, block_dofs)
    windows = jnp.concatenate(
        [segment[:, 0:block_rows], segment[:, 1 : block_rows + 1], segment[:, 2 : block_rows + 2]],
        axis=2,
    )
    band_view = near_band.reshape(block_rows, block_dofs, 3 * block_dofs)
    nearby = jnp.einsum("mik,idk->mid", windows, band_view, preferred_element_type=jnp.float32)
    return nearby.reshape(members, -1)


def local(stress, state, load_rate, a_param, b_param, near_band, u_far, v_far, ranks):
    row_index = lax.axis_index("row")
    col_index = lax.axis_index("col")
    row_ratio = lax.axis_size("row") // lax.axis_size("col")
    block_rows = u_far.shape[0]
    block_dofs = near_band.shape[1] // 3
    plate_rate = load_rate.astype(jnp.float32) * RATE_UNIT
    stress_start, state_start = (stress, state)

    def tendency(stress_now, state_now):
        excess, drift = rates_and_drift(stress_now, state_now, plate_rate, a_param, b_param)
        all_members = lax.all_gather(excess, "col", axis=0, tiled=True)
        owners = []
        for offset in range(row_ratio):
            owners.append(broadcast(all_members, "row", row_ratio * col_index + offset))
        columns = jnp.concatenate(owners, axis=1)
        partial_value = far_terms(columns, u_far, v_far, ranks, row_index, col_index)
        padded = extended(columns, (("col", 1),), block_dofs)
        on_band = col_index == row_index // row_ratio
        first_block = row_index % row_ratio * block_rows
        partial_value = partial_value + lax.cond(
            on_band,
            lambda: near_terms(padded, first_block, near_band),
            lambda: jnp.zeros_like(partial_value),
        )
        totals = lax.psum_scatter(partial_value, "col", scatter_dimension=0, tiled=True)
        return (-totals, drift)

    rate_one, drift_one = tendency(stress_start, state_start)
    stress_one = stress_start + HSTEP * rate_one
    state_one = state_start + HSTEP * drift_one
    rate_two, drift_two = tendency(stress_one, state_one)
    stress_two = 0.75 * stress_start + 0.25 * (stress_one + HSTEP * rate_two)
    state_two = 0.75 * state_start + 0.25 * (state_one + HSTEP * drift_two)
    rate_three, drift_three = tendency(stress_two, state_two)
    new_stress = stress_start / 3.0 + 2.0 / 3.0 * (stress_two + HSTEP * rate_three)
    new_state = state_start / 3.0 + 2.0 / 3.0 * (state_two + HSTEP * drift_three)
    return (new_stress, new_state)


def solution(mesh):
    return jax.shard_map(
        local,
        mesh=mesh,
        in_specs=(
            P("col", "row"),
            P("col", "row"),
            P("col", "row"),
            P("row"),
            P("row"),
            P("row", None),
            P("row", "col", None, None),
            P("row", "col", None, None),
            P("row", "col"),
        ),
        out_specs=(P("col", "row"), P("col", "row")),
        check_vma=False,
    )
```

profile of v0, /device:TPU:64, one launch (start us, length us, event | category | flops | bytes accessed | tf_op | source)
XLA Modules:
  0.0 1475.0 jit_solution(9471608002866167742)
XLA Ops:
  7.2 0.7 fusion.75
  8.0 0.7 div.62
  8.7 0.8 fusion.59
  9.6 43.9 %all_gather.9 = bf16[256,512]{1,0:T(8,128)(2,1)S(1)} all-gather(bf16[16,512]{1,0:T(8,128)(2,1)S(1)} %fusion.59), channel_id=1, replica_groups=mesh['row'=32,'col'=16] {'col'}, dimensions={0}, use_global_device_ids=true | all-gather | bytes 278528 | tf_op jit(solution)/shard_map/all_gather | solution.py:91
  53.4 0.9 broadcast_select_fusion.5
  54.4 0.1 abs_compare_fusion.3
  54.5 0.1 fusion.76
  54.6 336.6 %all-reduce.11.cloned.1.call-done = (bf16[256,512]{1,0:T(8,128)(2,1)}, bf16[256,512]{1,0:T(8,128)(2,1)}) async-done(((bf16[256,512]{1,0:T(8,128)(2,1)}, bf16[256,512]{1,0:T(8,128)(2,1)}), (bf16[256,512]{1,0:T(8,128)(2,1)}, bf16[256,512]{1,0:T(8,128)(2,1)})) %all-reduce.11.cloned.1.call-update) | async-done | bytes 524304 | tf_op jit(solution)/shard_map/psum | solution.py:13
  391.1 0.9 slice.60
  392.1 0.9 slice.61
  393.0 1.1 pad_maximum_fusion.3
  394.1 3.4 collective-permute-start
  397.5 1.3 collective-permute-start.1
  398.8 0.4 reshape.192
  399.2 0.5 fusion.29
  399.7 0.2 copy.27
  399.9 0.6 collective-permute-done
  400.5 4.1 collective-permute-done.1
  404.7 0.1 pad_maximum_fusion
  404.7 0.1 conditional.3
  404.8 0.1 broadcast.116.clone
  404.9 0.9 add.112
  405.9 0.2 multiply_reduce_fusion.2
  406.2 92.3 %reduce-scatter.4.cloned.1.call-done = f32[16,512]{1,0:T(8,128)} async-done(((f32[256,512]{1,0:T(8,128)}), f32[16,512]{1,0:T(8,128)}) %reduce-scatter.4.cloned.1.call-update) | async-done | bytes 32784 | tf_op jit(solution)/shard_map/reduce_scatter | solution.py:105
  498.5 0.8 fusion.58
  499.4 38.8 %all_gather.10 = bf16[256,512]{1,0:T(8,128)(2,1)S(1)} all-gather(bf16[16,512]{1,0:T(8,128)(2,1)S(1)} %get-tuple-element.58), channel_id=1, replica_groups=mesh['row'=32,'col'=16] {'col'}, dimensions={0}, use_global_device_ids=true | all-gather | bytes 278528 | tf_op jit(solution)/shard_map/all_gather | solution.py:91
  538.2 0.9 broadcast_select_fusion.4
  539.1 336.2 %all-reduce.9.cloned.1.call-done = (bf16[256,512]{1,0:T(8,128)(2,1)}, bf16[256,512]{1,0:T(8,128)(2,1)}) async-done(((bf16[256,512]{1,0:T(8,128)(2,1)}, bf16[256,512]{1,0:T(8,128)(2,1)}), (bf16[256,512]{1,0:T(8,128)(2,1)}, bf16[256,512]{1,0:T(8,128)(2,1)})) %all-reduce.9.cloned.1.call-update) | async-done | bytes 524304 | tf_op jit(solution)/shard_map/psum | solution.py:13
  875.3 0.9 slice.62
  876.2 0.9 slice.63
  877.1 1.1 pad_maximum_fusion.4
  878.2 3.4 collective-permute-start.2
  881.6 1.3 collective-permute-start.3
  882.9 0.4 reshape.194
  883.3 0.5 fusion.28
  883.8 0.2 copy.30
  884.0 0.7 collective-permute-done.2
  884.7 4.1 collective-permute-done.3
  888.8 0.1 pad_maximum_fusion.1
  888.8 0.1 conditional.4
  888.9 0.9 add.115
  889.9 0.2 multiply_reduce_fusion.1
  890.2 92.4 %reduce-scatter.6.cloned.1.call-done = f32[16,512]{1,0:T(8,128)} async-done(((f32[256,512]{1,0:T(8,128)}), f32[16,512]{1,0:T(8,128)}) %reduce-scatter.6.cloned.1.call-update) | async-done | bytes 32784 | tf_op jit(solution)/shard_map/reduce_scatter | solution.py:105
  982.7 0.8 fusion.57
  983.5 38.8 %all_gather.11 = bf16[256,512]{1,0:T(8,128)(2,1)S(1)} all-gather(bf16[16,512]{1,0:T(8,128)(2,1)S(1)} %get-tuple-element.56), channel_id=1, replica_groups=mesh['row'=32,'col'=16] {'col'}, dimensions={0}, use_global_device_ids=true | all-gather | bytes 278528 | tf_op jit(solution)/shard_map/all_gather | solution.py:91
  1022.3 0.9 broadcast_select_fusion.3
  1023.2 336.3 %all-reduce.7.cloned.1.call-done = (bf16[256,512]{1,0:T(8,128)(2,1)}, bf16[256,512]{1,0:T(8,128)(2,1)}) async-done(((bf16[256,512]{1,0:T(8,128)(2,1)}, bf16[256,512]{1,0:T(8,128)(2,1)}), (bf16[256,512]{1,0:T(8,128)(2,1)}, bf16[256,512]{1,0:T(8,128)(2,1)})) %all-reduce.7.cloned.1.call-update) | async-done | bytes 524304 | tf_op jit(solution)/shard_map/psum | solution.py:13
  1359.5 0.9 slice.64
  1360.5 0.9 slice.65
  1361.4 1.1 pad_maximum_fusion.5
  1362.5 3.4 collective-permute-start.4
  1365.9 1.3 collective-permute-start.5
  1367.2 0.4 reshape.196
  1367.5 0.5 fusion.27
  1368.1 0.2 copy.33
  1368.3 0.7 collective-permute-done.4
  1368.9 4.1 collective-permute-done.5
  1373.0 0.1 pad_maximum_fusion.2
  1373.1 0.1 conditional.5
  1373.2 0.9 add.120
  1374.1 0.2 multiply_reduce_fusion
  1374.3 0.6 fusion.64
  1375.0 91.8 %reduce-scatter.8.cloned.1.call-done = f32[16,512]{1,0:T(8,128)} async-done(((f32[256,512]{1,0:T(8,128)}), f32[16,512]{1,0:T(8,128)}) %reduce-scatter.8.cloned.1.call-update) | async-done | bytes 32784 | tf_op jit(solution)/shard_map/reduce_scatter | solution.py:105
  1466.7 1.4 multiply_add_fusion
  (63 shorter events, 0.9 us)
Async XLA Ops:
  7.2 392.0 %copy-start = (bf16[2,4,32,256]{3,2,1,0:T(8,128)(2,1)S(1)}, bf16[2,4,32,256]{3,2,1,0:T(8,128)(2,1)}, u32[]{:S(2)}) copy-start(bf16[2,4,32,256]{3,2,1,0:T(8,128)(2,1)} %param.21) | copy-start | bytes 393220
  7.2 384.0 %all-reduce.11.cloned.1.call-start = ((), (), s32[]{:S(2)}) async-start(), calls=%async_computation.8 | async-start | bytes 1048576 | tf_op jit(solution)/shard_map/psum | solution.py:13
  9.5 44.9 %copy-start.13 = (s32[2,4]{1,0:T(2,128)S(1)}, s32[2,4]{1,0:T(2,128)}, u32[]{:S(2)}) copy-start(s32[2,4]{1,0:T(2,128)} %param.23) | copy-start | bytes 100
  54.3 444.2 %reduce-scatter.4.cloned.1.call-start = ((), (), s32[]{:S(2)}) async-start(), calls=%async_computation.3 | async-start | bytes 557056 | tf_op jit(solution)/shard_map/reduce_scatter | solution.py:105
  393.0 6.2 copy-start.7
  394.1 6.4 collective-permute-start
  397.5 7.2 collective-permute-start.1
  399.7 5.0 copy-start.1
  399.7 5.0 copy-start.2
  399.9 4.8 copy-start.14
  404.8 1.0 copy-start.8
  404.8 1.0 copy-start.11
  404.8 1.2 copy-start.10
  404.9 1.2 copy-start.12
  405.8 92.8 %copy-start.9 = (s32[16,512]{1,0:T(8,128)S(1)}, s32[16,512]{1,0:T(8,128)}, u32[]{:S(2)}) copy-start(s32[16,512]{1,0:T(8,128)} %param.17) | copy-start | bytes 98308
  405.8 469.5 %all-reduce.9.cloned.1.call-start = ((), (), s32[]{:S(2)}) async-start(), calls=%async_computation.7 | async-start | bytes 1048576 | tf_op jit(solution)/shard_map/psum | solution.py:13
  539.1 443.6 %reduce-scatter.6.cloned.1.call-start = ((), (), s32[]{:S(2)}) async-start(), calls=%async_computation.4 | async-start | bytes 557056 | tf_op jit(solution)/shard_map/reduce_scatter | solution.py:105
  878.2 6.4 collective-permute-start.2
  881.6 7.2 collective-permute-start.3
  883.8 5.0 copy-start.5
  883.8 5.0 copy-start.6
  889.8 469.7 %all-reduce.7.cloned.1.call-start = ((), (), s32[]{:S(2)}) async-start(), calls=%async_computation.6 | async-start | bytes 1048576 | tf_op jit(solution)/shard_map/psum | solution.py:13
  1023.2 443.6 %reduce-scatter.8.cloned.1.call-start = ((), (), s32[]{:S(2)}) async-start(), calls=%async_computation.5 | async-start | bytes 557056 | tf_op jit(solution)/shard_map/reduce_scatter | solution.py:105
  1362.5 6.4 collective-permute-start.4
  1365.9 7.2 collective-permute-start.5
  1368.0 5.0 copy-start.3
  1368.0 5.0 copy-start.4
Sparse Core Ops, SparseCore 0:
  54.4 336.6 all-reduce.10
  405.9 92.5 reduce-scatter.3
  539.2 336.0 all-reduce.8
  890.0 92.6 reduce-scatter.5
  1023.3 336.2 all-reduce.6
  1374.2 92.4 reduce-scatter.7
where the time goes:
time: 1480 us; the launch traced here: 1470 us
  waiting for transfers between devices  1300 us (88%)
  blocking collectives  122 us (8%)
    psum x3, waiting for transfers between devices, broadcast(): return lax.psum(kept, axis)  1010 us
    reduce_scatter x3, waiting for transfers between devices, tendency(): lax.psum_scatter(partial_value, 'col', scatter_dimension=0, tiled=True)  277 us
    all_gather x3, blocking collectives, tendency(): all_members = lax.all_gather(excess, 'col', axis=0, tiled=True)  122 us
  transfers between devices with their start and end apart: 12, of which 12 were waited for; matrix products, arithmetic and copies ran while one was open for 0% of the time, Pallas kernels for 0%

commit v1 on v0

--- a/solution.py
+++ b/solution.py
@@ -10,7 +10,7 @@
 
 def broadcast(value, axis, source):
     kept = jnp.where(lax.axis_index(axis) == source, value, 0).astype(value.dtype)
-    return lax.psum(kept, axis)
+    return jnp.sum(lax.all_gather(kept, axis), axis=0)
 
 
 def extended(cells, sides, width):

time: 1480 us -> 1240 us (0.84)
  waiting for transfers between devices: 1300 us -> 1040 us
  other arithmetic: 14.6 us -> 39.9 us
    psum x3 -> x0, waiting for transfers between devices: 1010 us -> none  [broadcast(): return lax.psum(kept, axis)]
    all_gather x0 -> x6, waiting for transfers between devices: none -> 775 us  [broadcast(): return jnp.sum(lax.all_gather(kept, axis), axis=0)]
    reduce_sum x0 -> x6, other arithmetic: none -> 28.5 us  [broadcast(): return jnp.sum(lax.all_gather(kept, axis), axis=0)]
  transfers between devices with their start and end apart: 12 -> 15, of which waited for: 12 -> 15; matrix products, arithmetic and copies ran while one was open for 0% -> 1% of each run, Pallas kernels for 0% -> 0%
where the time goes in v1:
time: 1240 us
  waiting for transfers between devices  1040 us (84%)
  blocking collectives  122 us (10%)
  other arithmetic  39.9 us (3%)
  starting transfers between devices  18.1 us (1%)
  between operations  14.4 us (1%)
    all_gather x6, waiting for transfers between devices, broadcast(): return jnp.sum(lax.all_gather(kept, axis), axis=0)  775 us
    reduce_scatter x3, waiting for transfers between devices, tendency(): lax.psum_scatter(partial_value, 'col', scatter_dimension=0, tiled=True)  262 us
    all_gather x3, blocking collectives, tendency(): all_members = lax.all_gather(excess, 'col', axis=0, tiled=True)  122 us
    reduce_sum x6, other arithmetic, broadcast(): return jnp.sum(lax.all_gather(kept, axis), axis=0)  28.5 us
  transfers between devices with their start and end apart: 15, of which 15 were waited for; matrix products, arithmetic and copies ran while one was open for 1% of the time, Pallas kernels for 0%

profile of v1, /device:TPU:64, one launch (start us, length us, event | category | flops | bytes accessed | tf_op | source)
XLA Modules:
  0.0 1242.3 jit_solution(12327352037167102752)
XLA Ops:
  7.2 0.7 fusion.69
  8.1 0.7 div.62
  8.7 0.8 fusion.53
  9.6 43.9 %all_gather.45 = bf16[256,512]{1,0:T(8,128)(2,1)S(1)} all-gather(bf16[16,512]{1,0:T(8,128)(2,1)S(1)} %fusion.53), channel_id=1, replica_groups=mesh['row'=32,'col'=16] {'col'}, dimensions={0}, use_global_device_ids=true | all-gather | bytes 278528 | tf_op jit(solution)/shard_map/all_gather | solution.py:91
  53.4 0.8 broadcast_select_fusion.5
  54.3 0.7 all-gather.15.cloned.1.call-update
  55.1 0.1 abs_compare_fusion.3
  55.2 0.1 fusion.70
  55.3 131.7 %all-gather.13.cloned.1.call-done = bf16[8192,512]{1,0:T(8,128)(2,1)} async-done(((bf16[256,512]{1,0:T(8,128)(2,1)}), bf16[8192,512]{1,0:T(8,128)(2,1)}) %all-gather.13.cloned.1.call-update) | async-done | bytes 8388624 | tf_op jit(solution)/shard_map/all_gather | solution.py:13
  187.0 4.8 reduce_sum.99
  191.7 126.5 %all-gather.15.cloned.1.call-done = bf16[8192,512]{1,0:T(8,128)(2,1)} async-done(((bf16[256,512]{1,0:T(8,128)(2,1)}), bf16[8192,512]{1,0:T(8,128)(2,1)}) %all-gather.15.cloned.1.call-update) | async-done | bytes 8388624 | tf_op jit(solution)/shard_map/all_gather | solution.py:13
  318.3 4.8 reduce_sum.100
  323.2 1.3 collective-permute-start.1
  324.5 4.6 collective-permute-start
  329.0 0.2 copy.59
  329.3 0.4 fusion.29
  329.7 0.2 copy.62
  329.9 0.8 collective-permute-done.1
  330.7 1.2 collective-permute-done
  331.9 0.1 conditional.3
  332.1 0.9 add.100
  333.1 0.2 multiply_reduce_fusion.2
  333.4 87.4 %reduce-scatter.4.cloned.1.call-done = f32[16,512]{1,0:T(8,128)} async-done(((f32[256,512]{1,0:T(8,128)}), f32[16,512]{1,0:T(8,128)}) %reduce-scatter.4.cloned.1.call-update) | async-done | bytes 32784 | tf_op jit(solution)/shard_map/reduce_scatter | solution.py:105
  420.8 0.8 fusion.52
  421.6 38.8 %all_gather.50 = bf16[256,512]{1,0:T(8,128)(2,1)S(1)} all-gather(bf16[16,512]{1,0:T(8,128)(2,1)S(1)} %get-tuple-element.61), channel_id=1, replica_groups=mesh['row'=32,'col'=16] {'col'}, dimensions={0}, use_global_device_ids=true | all-gather | bytes 278528 | tf_op jit(solution)/shard_map/all_gather | solution.py:91
  460.5 0.8 broadcast_select_fusion.4
  461.3 0.5 all-gather.19.cloned.1.call-update
  461.9 132.0 %all-gather.17.cloned.1.call-done = bf16[8192,512]{1,0:T(8,128)(2,1)} async-done(((bf16[256,512]{1,0:T(8,128)(2,1)}), bf16[8192,512]{1,0:T(8,128)(2,1)}) %all-gather.17.cloned.1.call-update) | async-done | bytes 8388624 | tf_op jit(solution)/shard_map/all_gather | solution.py:13
  593.9 4.8 reduce_sum.102
  598.7 126.4 %all-gather.19.cloned.1.call-done = bf16[8192,512]{1,0:T(8,128)(2,1)} async-done(((bf16[256,512]{1,0:T(8,128)(2,1)}), bf16[8192,512]{1,0:T(8,128)(2,1)}) %all-gather.19.cloned.1.call-update) | async-done | bytes 8388624 | tf_op jit(solution)/shard_map/all_gather | solution.py:13
  725.1 4.8 reduce_sum.103
  729.9 1.3 collective-permute-start.3
  731.2 4.6 collective-permute-start.2
  735.8 0.2 copy.64
  736.0 0.4 fusion.28
  736.4 0.2 copy.67
  736.6 0.9 collective-permute-done.3
  737.5 1.2 collective-permute-done.2
  738.7 0.1 conditional.4
  738.8 0.9 add.103
  739.8 0.2 multiply_reduce_fusion.1
  740.1 87.4 %reduce-scatter.6.cloned.1.call-done = f32[16,512]{1,0:T(8,128)} async-done(((f32[256,512]{1,0:T(8,128)}), f32[16,512]{1,0:T(8,128)}) %reduce-scatter.6.cloned.1.call-update) | async-done | bytes 32784 | tf_op jit(solution)/shard_map/reduce_scatter | solution.py:105
  827.5 0.8 fusion.51
  828.3 38.8 %all_gather.55 = bf16[256,512]{1,0:T(8,128)(2,1)S(1)} all-gather(bf16[16,512]{1,0:T(8,128)(2,1)S(1)} %get-tuple-element.59), channel_id=1, replica_groups=mesh['row'=32,'col'=16] {'col'}, dimensions={0}, use_global_device_ids=true | all-gather | bytes 278528 | tf_op jit(solution)/shard_map/all_gather | solution.py:91
  867.2 0.8 broadcast_select_fusion.3
  868.1 0.7 all-gather.23.cloned.1.call-update
  868.8 0.2 reduce-scatter.8.cloned.1.call-start
  869.0 131.7 %all-gather.21.cloned.1.call-done = bf16[8192,512]{1,0:T(8,128)(2,1)} async-done(((bf16[256,512]{1,0:T(8,128)(2,1)}), bf16[8192,512]{1,0:T(8,128)(2,1)}) %all-gather.21.cloned.1.call-update) | async-done | bytes 8388624 | tf_op jit(solution)/shard_map/all_gather | solution.py:13
  1000.7 4.8 reduce_sum.105
  1005.5 126.5 %all-gather.23.cloned.1.call-done = bf16[8192,512]{1,0:T(8,128)(2,1)} async-done(((bf16[256,512]{1,0:T(8,128)(2,1)}), bf16[8192,512]{1,0:T(8,128)(2,1)}) %all-gather.23.cloned.1.call-update) | async-done | bytes 8388624 | tf_op jit(solution)/shard_map/all_gather | solution.py:13
  1132.0 4.8 reduce_sum.106
  1136.9 1.3 collective-permute-start.5
  1138.2 4.6 collective-permute-start.4
  1142.7 0.2 copy.69
  1142.9 0.4 fusion.27
  1143.4 0.2 copy.72
  1143.6 0.9 collective-permute-done.5
  1144.4 1.2 collective-permute-done.4
  1145.7 0.1 conditional.5
  1145.7 0.9 add.108
  1146.7 0.2 multiply_reduce_fusion
  1146.9 0.6 fusion.58
  1147.5 86.9 %reduce-scatter.8.cloned.1.call-done = f32[16,512]{1,0:T(8,128)} async-done(((f32[256,512]{1,0:T(8,128)}), f32[16,512]{1,0:T(8,128)}) %reduce-scatter.8.cloned.1.call-update) | async-done | bytes 32784 | tf_op jit(solution)/shard_map/reduce_scatter | solution.py:105
  1234.4 1.4 multiply_add_fusion
  (64 shorter events, 1.4 us)
Async XLA Ops:
  7.2 322.1 %copy-start = (bf16[2,4,32,256]{3,2,1,0:T(8,128)(2,1)S(1)}, bf16[2,4,32,256]{3,2,1,0:T(8,128)(2,1)}, u32[]{:S(2)}) copy-start(bf16[2,4,32,256]{3,2,1,0:T(8,128)(2,1)} %param.21) | copy-start | bytes 393220
  7.2 48.0 %copy-start.7 = (s32[2,4]{1,0:T(2,128)S(1)}, s32[2,4]{1,0:T(2,128)}, u32[]{:S(2)}) copy-start(s32[2,4]{1,0:T(2,128)} %param.23) | copy-start | bytes 100
  7.2 179.8 %all-gather.13.cloned.1.call-start = ((), (), s32[]{:S(2)}) async-start(), calls=%async_computation.6 | async-start | bytes 8650752 | tf_op jit(solution)/shard_map/all_gather | solution.py:13
  54.3 264.0 %all-gather.15.cloned.1.call-start = ((), (), s32[]{:S(2)}) async-start(), calls=%async_computation.7 | async-start | bytes 8650752 | tf_op jit(solution)/shard_map/all_gather | solution.py:13
  55.0 365.8 %reduce-scatter.4.cloned.1.call-start = ((), (), s32[]{:S(2)}) async-start(), calls=%async_computation.3 | async-start | bytes 557056 | tf_op jit(solution)/shard_map/reduce_scatter | solution.py:105
  323.0 6.2 copy-start.1
  323.2 7.5 collective-permute-start.1
  324.5 7.4 collective-permute-start
  332.0 1.0 copy-start.2
  332.0 1.0 copy-start.5
  332.0 1.2 copy-start.4
  332.1 1.2 copy-start.6
  332.1 88.7 %copy-start.3 = (s32[16,512]{1,0:T(8,128)S(1)}, s32[16,512]{1,0:T(8,128)}, u32[]{:S(2)}) copy-start(s32[16,512]{1,0:T(8,128)} %param.17) | copy-start | bytes 98308
  333.0 260.9 %all-gather.17.cloned.1.call-start = ((), (), s32[]{:S(2)}) async-start(), calls=%async_computation.8 | async-start | bytes 8650752 | tf_op jit(solution)/shard_map/all_gather | solution.py:13
  461.3 263.8 %all-gather.19.cloned.1.call-start = ((), (), s32[]{:S(2)}) async-start(), calls=%async_computation.9 | async-start | bytes 8650752 | tf_op jit(solution)/shard_map/all_gather | solution.py:13
  461.9 365.7 %reduce-scatter.6.cloned.1.call-start = ((), (), s32[]{:S(2)}) async-start(), calls=%async_computation.4 | async-start | bytes 557056 | tf_op jit(solution)/shard_map/reduce_scatter | solution.py:105
  729.9 7.5 collective-permute-start.3
  731.2 7.4 collective-permute-start.2
  739.7 261.0 %all-gather.21.cloned.1.call-start = ((), (), s32[]{:S(2)}) async-start(), calls=%async_computation.10 | async-start | bytes 8650752 | tf_op jit(solution)/shard_map/all_gather | solution.py:13
  868.0 264.0 %all-gather.23.cloned.1.call-start = ((), (), s32[]{:S(2)}) async-start(), calls=%async_computation.11 | async-start | bytes 8650752 | tf_op jit(solution)/shard_map/all_gather | solution.py:13
  868.8 365.6 %reduce-scatter.8.cloned.1.call-start = ((), (), s32[]{:S(2)}) async-start(), calls=%async_computation.5 | async-start | bytes 557056 | tf_op jit(solution)/shard_map/reduce_scatter | solution.py:105
  1136.9 7.5 collective-permute-start.5
  1138.2 7.4 collective-permute-start.4
Sparse Core Ops, SparseCore 0:
  54.4 132.5 all-gather.12
  190.3 127.8 all-gather.14
  333.1 87.6 reduce-scatter.3
  461.4 132.4 all-gather.16
  597.1 127.8 all-gather.18
  739.8 87.6 reduce-scatter.5
  868.1 132.5 all-gather.20
  1004.1 127.8 all-gather.22
  1146.8 87.6 reduce-scatter.7
